TPU v7x, 32 devices: a whole 2x2x4 slice. The times are simulated.
32 devices in a mesh: groups: 2 (over y), replica: 4 (over z), tensor: 4 (over x, core).
Axes of the slice: x: 2, y: 2, z: 4, core: 2. Of those that a mesh axis runs over, the one named last changes fastest.
Arguments:
- queries: bfloat16 [512, 64, 128], P(('groups', 'replica'), 'tensor'), parts along dimension 0, may hold values from -256 to 256
- prefix_pool: bfloat16 [16, 64, 2, 8, 128], P(('groups', 'replica'), None, None, 'tensor'), parts along dimension 0, may hold values from -8 to 8
- page_table: int32 [12], P('groups'), parts along dimension 0, may hold values from 0 to 7, as said below
- suffix_kv: bfloat16 [512, 24, 2, 8, 128], P(('groups', 'replica'), None, None, 'tensor'), parts along dimension 0, may hold values from -9 to 9
- new_kv: bfloat16 [512, 2, 8, 128], P(('groups', 'replica'), None, 'tensor'), parts along dimension 0, may hold values from -10 to 10
- suffix_len: int32 [512], P(('groups', 'replica')), parts along dimension 0, may hold values from 0 to 24
- counts: int32 [8], P(('groups', 'replica')), parts along dimension 0, may hold values from 0 to 64, as said below
Outputs:
- attended: bfloat16 [512, 64, 128], P(('groups', 'replica'), 'tensor'), parts along dimension 0
There are 2 independent parts, one for each index of `groups`. A program takes and returns all parts, laid end to end along the dimension named above; each array names one. Nothing has to cross between parts.
Inputs may be any that keep to these rules, and one draw needn't show every extreme that they name: `page_table`: 6 distinct pool slots, among them slots 0 and 7. The counts of replicas 2i and 2i + 1 sum to 64.
All inputs are finite; a program needn't handle non-finite values.
Results may differ from a plain program's by a relative error of at most 0.013.
Values may be sent and summed in bfloat16 or wider, within the bound.
A program may use at most 64 MiB of HBM per device.

v0:
```python
import math

import jax
import jax.numpy as jnp
from jax import lax
from jax.sharding import PartitionSpec as P

masked_score = -1e30


def empty_part(grouped):
    stat_shape = grouped.shape[:3]
    return (
        jnp.full(stat_shape, masked_score, jnp.float32),
        jnp.zeros(stat_shape, jnp.float32),
        jnp.zeros(grouped.shape, jnp.float32),
    )


def absorb(running, scores, contract):
    row_max = jnp.maximum(running[0], jnp.max(scores, axis=-1))
    factor = jnp.exp(running[0] - row_max)
    weights = jnp.exp(scores - row_max[..., None])
    row_total = running[1] * factor + jnp.sum(weights, axis=-1)
    accumulated = running[2] * factor[..., None] + contract(weights.astype(jnp.bfloat16))
    return (row_max, row_total, accumulated)


def merge_parts(earlier, later):
    row_max = jnp.maximum(earlier[0], later[0])
    scale_a = jnp.exp(earlier[0] - row_max)
    scale_b = jnp.exp(later[0] - row_max)
    row_total = earlier[1] * scale_a + later[1] * scale_b
    accumulated = earlier[2] * scale_a[..., None] + later[2] * scale_b[..., None]
    return (row_max, row_total, accumulated)


def fold_pages(running, grouped, piece, page_table):
    page_size = piece.shape[1]
    factor_q = grouped.shape[-1] ** (-0.5)
    slot_total = piece.shape[0]
    key_target = max(page_size, 32768 // grouped.shape[0])
    slot_block = math.gcd(slot_total, max(1, key_target // page_size))
    slot_ids = jnp.arange(slot_total, dtype=jnp.int32)
    live_slots = jnp.any(page_table[None, :] == slot_ids[:, None], axis=1)
    blocks = piece.reshape((slot_total // slot_block, slot_block * page_size) + piece.shape[2:])
    key_masks = jnp.repeat(
        live_slots.reshape(slot_total // slot_block, slot_block), page_size, axis=1
    )

    def absorb_block(inner_running, block_item):
        block, key_mask = block_item
        scores = (
            jnp.einsum("rgqd,kgd->rgqk", grouped, block[:, 0], preferred_element_type=jnp.float32)
            * factor_q
        )
        scores = jnp.where(key_mask[None, None, None, :], scores, masked_score)

        def contract(weights):
            return jnp.einsum(
                "rgqk,kgd->rgqd", weights, block[:, 1], preferred_element_type=jnp.float32
            )

        return (absorb(inner_running, scores, contract), None)

    result, unused = lax.scan(absorb_block, running, (blocks, key_masks))
    return result


def prefix_rows(grouped, prefix_pool, page_table):
    return fold_pages(
        empty_part(grouped),
        grouped,
        lax.all_gather(prefix_pool, "replica", axis=0, tiled=True),
        page_table,
    )


def suffix_part(grouped, suffix_kv, new_kv, suffix_len):
    factor_q = grouped.shape[-1] ** (-0.5)
    scores = (
        jnp.einsum(
            "rgqd,rkgd->rgqk", grouped, suffix_kv[:, :, 0], preferred_element_type=jnp.float32
        )
        * factor_q
    )
    kept_keys = jnp.arange(suffix_kv.shape[1], dtype=jnp.int32)[None, :] < suffix_len[:, None]
    scores = jnp.where(kept_keys[:, None, None, :], scores, masked_score)

    def contract_suffix(weights):
        return jnp.einsum(
            "rgqk,rkgd->rgqd", weights, suffix_kv[:, :, 1], preferred_element_type=jnp.float32
        )

    running = absorb(empty_part(grouped), scores, contract_suffix)
    fresh_score = (
        jnp.einsum("rgqd,rgd->rgq", grouped, new_kv[:, 0], preferred_element_type=jnp.float32)
        * factor_q
    )

    def contract_new(weights):
        return jnp.einsum(
            "rgqk,rgd->rgqd", weights, new_kv[:, 1], preferred_element_type=jnp.float32
        )

    return absorb(running, fresh_score[..., None], contract_new)


def shards(queries, prefix_pool, page_table, suffix_kv, new_kv, suffix_len, counts):
    slot_rows = queries.shape[0]
    head_count = queries.shape[1]
    kv_heads = prefix_pool.shape[3]
    grouped = queries.reshape(slot_rows, kv_heads, head_count // kv_heads, queries.shape[2])
    slot_count = counts[0]
    prefix = prefix_rows(grouped, prefix_pool, page_table)
    combined = merge_parts(prefix, suffix_part(grouped, suffix_kv, new_kv, suffix_len))
    result = combined[2] / combined[1][..., None]
    live_rows = jnp.arange(slot_rows, dtype=jnp.int32) < slot_count
    result = jnp.where(live_rows[:, None, None, None], result, 0.0)
    return result.reshape(slot_rows, head_count, queries.shape[2]).astype(jnp.bfloat16)


def solution(mesh):
    placed = (
        P(("groups", "replica"), "tensor", None),
        P(("groups", "replica"), None, None, "tensor", None),
        P("groups"),
        P(("groups", "replica"), None, None, "tensor", None),
        P(("groups", "replica"), None, "tensor", None),
        P(("groups", "replica")),
        P(("groups", "replica")),
    )
    return jax.shard_map(
        shards,
        mesh=mesh,
        in_specs=placed,
        out_specs=P(("groups", "replica"), "tensor", None),
        check_vma=False,
    )
```

profile of v0, /device:TPU:0, one launch (start us, length us, event | category | flops | bytes accessed | tf_op | source)
XLA Modules:
  0.0 32.1 jit_solution(2898645343890755833)
XLA Ops:
  0.0 0.0 copy-start
  0.0 1.0 %copy.75 = bf16[2,64,2,2,128]{4,1,3,2,0:T(8,128)(2,1)S(1)} copy(bf16[2,64,2,2,128]{4,3,2,1,0:T(2,128)(2,1)} %param.8) | data formatting | bytes 262144 | tf_op args[1]
  1.0 17.4 %all_gather.3 = bf16[8,64,2,2,128]{4,1,3,2,0:T(8,128)(2,1)S(1)} all-gather(bf16[2,64,2,2,128]{4,1,3,2,0:T(8,128)(2,1)S(1)} %copy.75), channel_id=1, replica_groups=mesh['groups'=2,'replica'=4,'tensor'=4] {'replica'}, dimensions={0}, use_global_device_ids=true | all-gather | bytes 655360 | tf_op jit(solution)/shard_map/all_gather | solution.py:74
  18.4 0.8 %fusion.26 = pred[8]{0:T(512)(128)(4,1)S(1)} fusion(s32[6]{0:T(128)} %param.9), kind=kLoop, calls=%fused_computation.52 | loop fusion | flops 88 | bytes 32 | tf_op jit(solution)/shard_map/reduce_or | solution.py:45
  19.2 0.1 broadcast_in_dim.64
  19.2 0.1 broadcast_in_dim.65
  19.3 0.0 copy-done
  19.3 0.5 %bitcast_reduce_fusion = (f32[64,2,8]{0,2,1:T(8,128)S(1)}, f32[2,512,64,8]{1,2,3,0:T(8,128)S(1)}) fusion(pred[512]{0:T(512)(128)(4,1)S(1)} %broadcast_in_dim.65, bf16[64,2,8,128]{3,2,1,0:T(8,128)(2,1)S(1)} %bitcast.91, bf16[512,2,2,128]{3,0,2,1:T(8,128)(2,1)S(1)} %bitcast.92), kind=kOutput, calls=%fused_computation.1 | convolution fusion | flops 135789568 | bytes 2626048 | tf_op jit(solution)/shard_map/while/body/eval_jaxpr/rgqd,kgd->rgqk/dot_general | solution.py:54
  19.9 0.0 copy-start.1
  19.9 1.3 %fusion.1 = (f32[64,2,8]{0,2,1:T(8,128)}, bf16[64,2,8,512]{3,0,2,1:T(8,128)(2,1)S(1)}) fusion(f32[2,512,64,8]{1,2,3,0:T(8,128)S(1)} %get-tuple-element.44, f32[64,2,8]{0,2,1:T(8,128)S(1)} %broadcast_maximum_fusion.1, pred[512]{0:T(512)(128)(4,1)S(1)} %broadcast_in_dim.65), kind=kLoop, calls=%fused_computation.4 | loop fusion | flops 2620416 | bytes 3154432 | tf_op jit(solution)/shard_map/while/body/eval_jaxpr/reduce_sum | solution.py:24
  21.1 0.1 copy-done.1
  21.3 1.1 %fusion.29 = (bf16[64,24,1,2,128]{4,3,2,1,0:T(2,128)(2,1)S(1)}, bf16[64,24,1,2,128]{4,3,2,1,0:T(2,128)(2,1)S(1)}) fusion(bf16[64,24,2,2,128]{4,3,2,1,0:T(2,128)(2,1)S(1)} %copy-done.1), kind=kLoop, calls=%fused_computation.56 | loop fusion | bytes 3145728 | tf_op jit(solution)/shard_map/slice | solution.py:83
  22.4 0.1 iota_compare_fusion
  22.4 0.7 %fusion.30 = (f32[64,2,8]{2,1,0:T(2,128)S(1)}, f32[64,2,8,24]{3,2,1,0:T(8,128)S(1)}) fusion(bf16[64,24,1,2,128]{4,3,2,1,0:T(2,128)(2,1)S(1)} %get-tuple-element.19, bf16[64,16,128]{2,1,0:T(8,128)(2,1)S(1)} %copy-done, pred[64,24]{1,0:T(8,128)(4,1)S(1)} %iota_compare_fusion), kind=kOutput, calls=%fused_computation.57 | convolution fusion | flops 6364160 | bytes 1152512 | tf_op jit(solution)/shard_map/rgqd,rkgd->rgqk/dot_general | solution.py:82
  23.1 0.1 copy.81
  23.2 0.1 copy.84
  23.3 0.4 %fusion.16 = (f32[64,2,8]{2,1,0:T(2,128)S(1)}, bf16[64,2,8,24]{3,2,1,0:T(8,128)(2,1)S(1)}) fusion(f32[64,2,8,24]{3,2,1,0:T(8,128)S(1)} %get-tuple-element.42, f32[64,2,8]{2,1,0:T(2,128)S(1)} %copy.84), kind=kLoop, calls=%fused_computation.24 | loop fusion | flops 72704 | bytes 155648 | tf_op jit(solution)/shard_map/reduce_sum | solution.py:24
  23.8 0.1 copy.91
  23.8 0.8 %bitcast_convert_fusion = (f32[64,2,128]{2,1,0:T(2,128)S(1)}, bf16[64,2,128,1]{2,1,0,3:T(2,128)(2,1)S(1)}) fusion(bf16[64,2,2,128]{3,2,1,0:T(2,128)(2,1)} %param.11), kind=kLoop, calls=%fused_computation.34 | loop fusion | flops 16384 | bytes 163840 | tf_op jit(solution)/shard_map/convert.3
  24.7 0.3 fusion.21
  24.9 0.1 copy.97
  25.0 0.7 %fusion.23 = (f32[64,2,8]{0,2,1:T(8,128)S(1)}, f32[64,2,8]{0,2,1:T(8,128)S(1)}, f32[64,2,8]{0,2,1:T(8,128)S(1)}, f32[64,2,8]{0,2,1:T(8,128)S(1)}, f32[64,2,8]{0,...) fusion(f32[64,2,1,8]{0,3,1,2:T(8,128)S(1)} %copy.97, f32[64,2,8]{0,2,1:T(8,128)S(1)} %get-tuple-element.43, ...), kind=kLoop, calls=%fused_computation.39 | loop fusion | flops 22528 | bytes 49152 | tf_op jit(solution)/shard_map/exp | solution.py:31
  25.8 0.1 copy.83
  25.8 0.1 copy.87
  25.9 0.1 copy.88
  26.1 0.1 copy.90
  26.2 1.5 %fusion.11 = f32[64,2,8,128]{3,2,0,1:T(8,128)} fusion(bf16[64,24,1,2,128]{4,3,2,1,0:T(2,128)(2,1)S(1)} %get-tuple-element.20, bf16[64,2,8,24]{3,2,1,0:T(8,128)(2,1)S(1)} %get-tuple-element.30, f32[64,2,8]{2,0,1:T(8,128)S(1)} %copy.90, f32[64,2,128]{2,0,1:T(8,128)S(1)} %copy.89, f32[64,2,8]{2,0,1:T(8,128)S(1)} %copy.88, f32[64,2,8]{2,0,1:T(8,128)S(1)} %copy.87, ...), kind=kOutput, calls=%fused_computation.17 | convolution fusion | flops 6946816 | bytes 1441792 | tf_op jit(solution)/shard_map/rgqk,rkgd->rgqd/dot_general | solution.py:91
  27.7 0.1 copy.78
  27.8 0.1 copy.82
  27.9 0.1 copy.92
  28.6 2.7 %fusion.12 = bf16[64,2,8,128]{3,2,0,1:T(8,128)(2,1)S(1)} fusion(f32[64,2,8,128]{3,2,0,1:T(8,128)} %fusion.11, bf16[64,2,8,512]{3,0,2,1:T(8,128)(2,1)S(1)} %get-tuple-element.18, bf16[512,2,2,128]{3,0,2,1:T(8,128)(2,1)S(1)} %bitcast.93, f32[64,2,8]{2,0,1:T(8,128)S(1)} %copy.92, f32[64,2,8]{2,0,1:T(8,128)S(1)} %copy.82, f32[64,2,8]{2,0,1:T(8,128)S(1)} %copy.78, ...), kind=kOutput, calls=%fused_computation.18 | convolution fusion | flops 135004160 | bytes 2294272 | tf_op jit(solution)/shard_map/while/body/eval_jaxpr/rgqk,kgd->rgqd/dot_general | solution.py:60
  31.3 0.7 %copy.123 = bf16[64,2,8,128]{3,2,1,0:T(8,128)(2,1)} copy(bf16[64,2,8,128]{3,2,0,1:T(8,128)(2,1)S(1)} %fusion.12) | data formatting | bytes 524288 | tf_op jit(solution)/shard_map/convert_element_type | solution.py:120
  (7 shorter events, 0.1 us)
Async XLA Ops:
  0.0 19.3 %copy-start = (bf16[64,16,128]{2,1,0:T(8,128)(2,1)S(1)}, bf16[64,16,128]{2,1,0:T(8,128)(2,1)}, u32[]{:S(2)}) copy-start(bf16[64,16,128]{2,1,0:T(8,128)(2,1)} %param.7) | copy-start | bytes 786436
  19.9 1.4 %copy-start.1 = (bf16[64,24,2,2,128]{4,3,2,1,0:T(2,128)(2,1)S(1)}, bf16[64,24,2,2,128]{4,3,2,1,0:T(2,128)(2,1)}, u32[]{:S(2)}) copy-start(bf16[64,24,2,2,128]{4,3,2,1,0:T(2,128)(2,1)} %param.10) | copy-start | bytes 4718596
  21.1 1.2 %copy-start.2 = (s32[64]{0:T(128)S(1)}, s32[64]{0:T(128)}, u32[]{:S(2)}) copy-start(s32[64]{0:T(128)} %param.12) | copy-start | bytes 772
where the time goes:
time: 32.4 us; the launch traced here: 32.1 us
  blocking collectives  17.4 us (54%)
  matrix products  5.68 us (18%)
  local copies, waits for them, and re-layouts  4.11 us (13%)
  other arithmetic  4.1 us (13%)
  between operations  0.81 us (2%)
    all_gather x1, blocking collectives, prefix_rows(): lax.all_gather(prefix_pool, 'replica', axis=0, tiled=True)  17.4 us
    dot_general x1, matrix products, contract(): jnp.einsum('rgqk,kgd->rgqd', weights, block[:, 1], preferred_element_type...  2.66 us
    reduce_sum x2, other arithmetic, absorb(): row_total = running[1] * factor + jnp.sum(weights, axis=-1)  1.67 us
    dot_general x1, matrix products, contract_suffix(): jnp.einsum('rgqk,rkgd->rgqd', weights, suffix_kv[:, :, 1], preferred_elem...  1.51 us
    unnamed x7, local copies, waits for them, and re-layouts  1.11 us
    slice x1, local copies, waits for them, and re-layouts, suffix_part(): suffix_kv[:, :, 0]  1.08 us
    another operation x1, other arithmetic  0.83 us
    reduce_or x1, other arithmetic, fold_pages(): live_slots = jnp.any(page_table[None, :] == slot_ids[:, None], axis=1)  0.77 us

commit v1 on v0

v1 whole, which is shorter than its diff:
```python
import functools
import math

import jax
import jax.numpy as jnp
from jax import lax
from jax.experimental import pallas as pl
from jax.experimental.pallas import tpu as pltpu
from jax.sharding import PartitionSpec as P

masked_score = -1e30
MESH = pl.DeviceIdType.MESH
SB = 8


def kernel(n, dims, table_ref, len_ref, count_ref, q_hbm, pool_hbm, suf_hbm, new_hbm, out_ref,
           gather, q_in, suf, new, perm, qs, knew, vnew, kx, vx, m_ref, acc_ref,
           local_sem, send_sem, recv_sem):
    rows, heads, kv_heads, depth, suf_len, page, slots, chunks = dims
    group = heads // kv_heads
    per_token = 2 * kv_heads
    scale = (1.0 / math.sqrt(depth)) * math.log2(math.e)
    block_rows = slots * page * per_token
    chunk_rows = block_rows // chunks
    tile_tokens = page
    tile_rows = page * per_token
    keys = slots * page
    me = lax.axis_index("replica")
    has_left, has_right = me > 0, me < n - 1

    barrier = pltpu.get_barrier_semaphore()

    @pl.when(has_left)
    def _():
        pl.semaphore_signal(barrier, inc=1, device_id={"replica": me - 1}, device_id_type=MESH)

    @pl.when(has_right)
    def _():
        pl.semaphore_signal(barrier, inc=1, device_id={"replica": me + 1}, device_id_type=MESH)

    copies = [
        pltpu.make_async_copy(q_hbm, q_in, local_sem.at[0]),
        pltpu.make_async_copy(new_hbm, new, local_sem.at[1]),
        pltpu.make_async_copy(suf_hbm, suf, local_sem.at[2]),
        pltpu.make_async_copy(pool_hbm, gather.at[me], local_sem.at[3]),
    ]
    for copy in copies:
        copy.start()

    out_row = lax.broadcasted_iota(jnp.int32, (tile_rows, tile_rows), 0)
    in_row = lax.broadcasted_iota(jnp.int32, (tile_rows, tile_rows), 1)
    source = lax.rem(out_row, page) * per_token + lax.div(out_row, page)
    perm[...] = jnp.where(in_row == source, 1.0, 0.0).astype(jnp.bfloat16)

    pl.semaphore_wait(barrier, has_left.astype(jnp.int32) + has_right.astype(jnp.int32))

    def send(direction, block, chunk, own):
        at = pl.ds(chunk * chunk_rows, chunk_rows)
        return pltpu.make_async_remote_copy(
            src_ref=pool_hbm.at[at] if own else gather.at[block, at],
            dst_ref=gather.at[block, at],
            send_sem=send_sem.at[direction, block, chunk],
            recv_sem=recv_sem.at[block, chunk],
            device_id={"replica": me + 1 if direction == 0 else me - 1},
            device_id_type=MESH,
        )

    for chunk in range(chunks):
        @pl.when(has_right)
        def _():
            send(0, me, chunk, True).start()

        @pl.when(has_left)
        def _():
            send(1, me, chunk, True).start()

    def relay(step, chunk):
        @pl.when(me - step >= 0)
        def _():
            send(0, me - step, chunk, False).wait_recv()

            @pl.when(has_right)
            def _():
                send(0, me - step, chunk, False).start()

        @pl.when(me + step < n)
        def _():
            send(1, me + step, chunk, False).wait_recv()

            @pl.when(has_left)
            def _():
                send(1, me + step, chunk, False).start()

    def split(block):
        return jnp.dot(perm[...], block, preferred_element_type=jnp.float32).astype(jnp.bfloat16)

    def piece(parts, which, head):
        at = (which * kv_heads + head) * page
        return parts[at : at + page]

    copies[0].wait()
    copies[1].wait()
    queries = q_in[...].astype(jnp.float32).reshape(rows, kv_heads, group, depth)
    for head in range(kv_heads):
        qs[head] = queries[:, head].reshape(rows * group, depth).astype(jnp.bfloat16)
    fresh = split(new[...])
    for head in range(kv_heads):
        knew[head] = piece(fresh, 0, head)
        vnew[head] = piece(fresh, 1, head)
    copies[2].wait()

    block_keys = SB * suf_len
    width = block_keys + rows
    tiles = block_keys // tile_tokens
    part = SB * group

    def suffix_block(index):
        columns = lax.broadcasted_iota(jnp.int32, (group, width), 1)
        masks = []
        for at in range(SB):
            low = at * suf_len
            high = low + len_ref[index * SB + at]
            own = (columns >= low) & (columns < high)
            masks.append(own | (columns == block_keys + index * SB + at))
        parts = [
            split(suf[pl.ds(pl.multiple_of((index * tiles + t) * tile_rows, tile_rows), tile_rows), :])
            for t in range(tiles)
        ]
        ones = jnp.ones((width, depth), jnp.bfloat16)
        at = pl.ds(pl.multiple_of(index * part, part), part)
        for head in range(kv_heads):
            key = jnp.concatenate([piece(p, 0, head) for p in parts] + [knew[head]], axis=0)
            value = jnp.concatenate([piece(p, 1, head) for p in parts] + [vnew[head]], axis=0)
            value = jnp.concatenate([value, ones], axis=1)
            scores = lax.dot_general(
                qs[head, at, :], key, (((1,), (1,)), ((), ())), preferred_element_type=jnp.float32
            )
            scores = jnp.concatenate(
                [
                    jnp.where(masks[i], scores[i * group : (i + 1) * group], masked_score)
                    for i in range(SB)
                ],
                axis=0,
            )
            top = jnp.max(scores, axis=1, keepdims=True)
            weights = jnp.exp2((scores - top) * scale).astype(jnp.bfloat16)
            acc_ref[head, at, :] = jnp.dot(weights, value, preferred_element_type=jnp.float32)
            m_ref[head, at, :] = jnp.broadcast_to(top, (part, depth))

    def prepare(side, block):
        parts = [split(gather[block, s * tile_rows : (s + 1) * tile_rows, :]) for s in range(slots)]
        for head in range(kv_heads):
            kx[side, head] = jnp.concatenate([piece(p, 0, head) for p in parts], axis=0)
            vx[side, head, :, :depth] = jnp.concatenate([piece(p, 1, head) for p in parts], axis=0)

    def slot_live(slot):
        def look(at, found):
            return found | (table_ref[at] == slot).astype(jnp.int32)

        pages = table_ref.shape[0]
        if pages <= 16:
            found = jnp.int32(0)
            for at in range(pages):
                found = look(at, found)
            return found
        return lax.fori_loop(0, pages, look, jnp.int32(0))

    quarter = rows * group // chunks

    def prefix_part(side, block, which):
        columns = lax.broadcasted_iota(jnp.int32, (1, keys), 1)
        live = jnp.zeros((1, keys), jnp.int32)
        for s in range(slots):
            inside = (columns >= s * page) & (columns < (s + 1) * page)
            live = jnp.where(inside, slot_live(block * slots + s), live)
        at = pl.ds(which * quarter, quarter)
        for head in range(kv_heads):
            scores = lax.dot_general(
                qs[head, at, :], kx[side, head], (((1,), (1,)), ((), ())),
                preferred_element_type=jnp.float32,
            )
            scores = jnp.where(live > 0, scores, masked_score)
            before = m_ref[head, at, :]
            top = jnp.maximum(before, jnp.max(scores, axis=1, keepdims=True))
            factor = jnp.exp2((before - top) * scale)
            weights = jnp.exp2((scores - top[:, :1]) * scale).astype(jnp.bfloat16)
            added = jnp.dot(weights, vx[side, head], preferred_element_type=jnp.float32)
            acc_ref[head, at, :depth] = acc_ref[head, at, :depth] * factor + added[:, :depth]
            acc_ref[head, at, depth:] = acc_ref[head, at, depth:] * factor + added[:, depth:]
            m_ref[head, at, :] = top

    def absorb(step, which):
        if isinstance(step, int) and step == 0:
            if which == 0:
                prepare(0, me)
            prefix_part(0, me, which)
            return

        @pl.when(me - step >= 0)
        def _():
            if which == 0:
                prepare(0, me - step)
            prefix_part(0, me - step, which)

        @pl.when(me + step < n)
        def _():
            if which == 0:
                prepare(1, me + step)
            prefix_part(1, me + step, which)

    for side in range(2):
        for head in range(kv_heads):
            vx[side, head, :, depth:] = jnp.ones((keys, depth), jnp.bfloat16)

    suffix_blocks = rows // SB
    early = suffix_blocks // 2
    late = (suffix_blocks - early) // chunks

    def run_suffix(first, count):
        def body(index, carry):
            suffix_block(first + index)
            return carry

        lax.fori_loop(0, count, body, 0)

    run_suffix(0, suffix_blocks - late * chunks)
    copies[3].wait()
    for chunk in range(chunks):
        relay(1, chunk)
        run_suffix(suffix_blocks - late * (chunks - chunk), late)
    for chunk in range(chunks):
        absorb(0, chunk)

    def step_body(step):
        for chunk in range(chunks):
            relay(step, chunk)
            absorb(step - 1, chunk)

    if n <= 8:
        for step in range(2, n):
            step_body(step)
    else:
        def loop(step, carry):
            step_body(step)
            return carry

        lax.fori_loop(2, n, loop, 0)
    for chunk in range(chunks):
        absorb(n - 1, chunk)

    span = rows // chunks
    count = count_ref[0]
    for chunk in range(chunks):
        at = pl.ds(chunk * quarter, quarter)
        heads_out = [
            (acc_ref[head, at, :depth] / acc_ref[head, at, depth:]).reshape(span, group, depth)
            for head in range(kv_heads)
        ]
        result = jnp.concatenate(heads_out, axis=1)
        row = lax.broadcasted_iota(jnp.int32, result.shape, 0) + chunk * span
        result = jnp.where(row < count, result, 0.0)
        out_ref[pl.ds(chunk * span, span)] = result.astype(jnp.bfloat16)

    def drain(block):
        for chunk in range(chunks):
            @pl.when(has_right & (block <= me))
            def _():
                send(0, block, chunk, False).wait_send()

            @pl.when(has_left & (block >= me))
            def _():
                send(1, block, chunk, False).wait_send()

    if n <= 8:
        for block in range(n):
            drain(block)
    else:
        def drain_loop(block, carry):
            drain(block)
            return carry

        lax.fori_loop(0, n, drain_loop, 0)


def shards(n, queries, prefix_pool, page_table, suffix_kv, new_kv, suffix_len, counts):
    rows, heads, depth = queries.shape
    slots, page, pair, kv_heads, depth = prefix_pool.shape
    suf_len = suffix_kv.shape[1]
    chunks = 4 if n <= 8 else 2
    group = heads // kv_heads
    dims = (rows, heads, kv_heads, depth, suf_len, page, slots, chunks)
    pool = prefix_pool.reshape(slots * page * 2 * kv_heads, depth)
    suffix = suffix_kv.reshape(rows * suf_len * 2 * kv_heads, depth)
    new = new_kv.reshape(rows * 2 * kv_heads, depth)
    tile_rows = page * 2 * kv_heads
    bf, f32 = jnp.bfloat16, jnp.float32
    anywhere = pl.BlockSpec(memory_space=pl.ANY)
    scalars = pl.BlockSpec(memory_space=pltpu.SMEM)
    return pl.pallas_call(
        functools.partial(kernel, n, dims),
        name="attend",
        out_shape=jax.ShapeDtypeStruct((rows, heads, depth), bf),
        in_specs=[scalars] * 3 + [anywhere] * 4,
        out_specs=pl.BlockSpec(memory_space=pltpu.VMEM),
        scratch_shapes=[
            pltpu.VMEM((n,) + pool.shape, bf),
            pltpu.VMEM(queries.shape, bf),
            pltpu.VMEM(suffix.shape, bf),
            pltpu.VMEM(new.shape, bf),
            pltpu.VMEM((tile_rows, tile_rows), bf),
            pltpu.VMEM((kv_heads, rows * group, depth), bf),
            pltpu.VMEM((kv_heads, rows, depth), bf),
            pltpu.VMEM((kv_heads, rows, depth), bf),
            pltpu.VMEM((2, kv_heads, slots * page, depth), bf),
            pltpu.VMEM((2, kv_heads, slots * page, 2 * depth), bf),
            pltpu.VMEM((kv_heads, rows * group, depth), f32),
            pltpu.VMEM((kv_heads, rows * group, 2 * depth), f32),
            pltpu.SemaphoreType.DMA((4,)),
            pltpu.SemaphoreType.DMA((2, n, chunks)),
            pltpu.SemaphoreType.DMA((n, chunks)),
        ],
        compiler_params=pltpu.CompilerParams(collective_id=0, has_side_effects=True),
    )(page_table, suffix_len, counts, queries, pool, suffix, new)


def solution(mesh):
    placed = (
        P(("groups", "replica"), "tensor", None),
        P(("groups", "replica"), None, None, "tensor", None),
        P("groups"),
        P(("groups", "replica"), None, None, "tensor", None),
        P(("groups", "replica"), None, "tensor", None),
        P(("groups", "replica")),
        P(("groups", "replica")),
    )
    return jax.shard_map(
        functools.partial(shards, mesh.shape["replica"]),
        mesh=mesh,
        in_specs=placed,
        out_specs=P(("groups", "replica"), "tensor", None),
        check_vma=False,
    )
```

time: 32.4 us -> 26.9 us (0.83)
  Pallas kernels: 0 us -> 24.4 us
  blocking collectives: 17.4 us -> 0 us
  matrix products: 5.68 us -> 0 us
  other arithmetic: 4.1 us -> 0 us
  local copies, waits for them, and re-layouts: 4.11 us -> 1.67 us
    pallas_call x0 -> x1, Pallas kernels: none -> 24.4 us  [shards(): pl.pallas_call(functools.partial(kernel, n, dims), name='attend', out_sha...]
    all_gather x1 -> x0, blocking collectives: 17.4 us -> none  [prefix_rows(): lax.all_gather(prefix_pool, 'replica', axis=0, tiled=True)]
    dot_general x5 -> x0, matrix products: 5.68 us -> none  [the longest x1 2.66 us: contract(): jnp.einsum('rgqk,kgd->rgqd', weights, block[:, 1], preferred_element_type...]
    reduce_sum x2 -> x0, other arithmetic: 1.67 us -> none  [absorb(): row_total = running[1] * factor + jnp.sum(weights, axis=-1)]
    slice x1 -> x0, local copies, waits for them, and re-layouts: 1.08 us -> none  [suffix_part(): suffix_kv[:, :, 0]]
    another operation x2 -> x0, other arithmetic: 0.84 us -> none
    reduce_or x1 -> x0, other arithmetic: 0.77 us -> none  [fold_pages(): live_slots = jnp.any(page_table[None, :] == slot_ids[:, None], axis=1)]
    convert_element_type x1 -> x0, local copies, waits for them, and re-layouts: 0.75 us -> none  [shards(): result.reshape(slot_rows, head_count, queries.shape[2]).astype(jnp.bfloat16)]
where the time goes in v1:
time: 26.9 us; the launch traced here: 26.8 us
  Pallas kernels  24.4 us (91%)
  local copies, waits for them, and re-layouts  1.67 us (6%)
  between operations  0.66 us (2%)
    pallas_call x1, Pallas kernels, shards(): pl.pallas_call(functools.partial(kernel, n, dims), name='attend', out_sha...  24.4 us
    unnamed x1, local copies, waits for them, and re-layouts  1.67 us

profile of v1, /device:TPU:0, one launch (start us, length us, event | category | flops | bytes accessed | tf_op | source)
XLA Modules:
  0.0 26.8 jit_solution(11032814132364288293)
XLA Ops:
  0.7 24.4 %attend.1 = bf16[64,16,128]{2,1,0:T(8,128)(2,1)} custom-call(s32[6]{0:T(128)} %table_ref.1, s32[64]{0:T(128)} %len_ref.1, s32[1]{0:T(128)S(6)} %copy.9.count_ref, bf16[64,16,128]{2,1,0:T(8,128)(2,1)} %q_hbm.1, bf16[512,128]{1,0:T(8,128)(2,1)} %bitcast.4, bf16[6144,128]{1,0:T(8,128)(2,1)} %bitcast.3, bf16[256,128]{1,0:T(8,128)(2,1)} %bitcast.5), custom_call_target="tpu_custom_call" | custom-call | tf_op jit(solution)/shard_map/attend/pallas_call | solution.py:299
  25.1 1.7 %copy.10 = bf16[64,16,128]{2,1,0:T(8,128)(2,1)} copy(bf16[64,16,128]{2,1,0:T(8,128)(2,1)} %attend.1) | data formatting | bytes 524288

commit v2 on v1

--- a/solution.py
+++ b/solution.py
@@ -13,8 +13,8 @@
 SB = 8
 
 
-def kernel(n, dims, table_ref, len_ref, count_ref, q_hbm, pool_hbm, suf_hbm, new_hbm, out_ref,
-           gather, q_in, suf, new, perm, qs, knew, vnew, kx, vx, m_ref, acc_ref,
+def kernel(n, dims, table_hbm, len_hbm, count_hbm, q_hbm, pool_hbm, suf_hbm, new_hbm, out_ref,
+           table_ref, len_ref, count_ref, gather, q_in, suf, new, perm, qs, knew, vnew, kx, vx, m_ref, acc_ref,
            local_sem, send_sem, recv_sem):
     rows, heads, kv_heads, depth, suf_len, page, slots, chunks = dims
     group = heads // kv_heads
@@ -43,6 +43,9 @@
         pltpu.make_async_copy(new_hbm, new, local_sem.at[1]),
         pltpu.make_async_copy(suf_hbm, suf, local_sem.at[2]),
         pltpu.make_async_copy(pool_hbm, gather.at[me], local_sem.at[3]),
+        pltpu.make_async_copy(table_hbm, table_ref, local_sem.at[4]),
+        pltpu.make_async_copy(len_hbm, len_ref, local_sem.at[5]),
+        pltpu.make_async_copy(count_hbm, count_ref, local_sem.at[6]),
     ]
     for copy in copies:
         copy.start()
@@ -108,6 +111,8 @@
         knew[head] = piece(fresh, 0, head)
         vnew[head] = piece(fresh, 1, head)
     copies[2].wait()
+    for copy in copies[4:]:
+        copy.wait()
 
     block_keys = SB * suf_len
     width = block_keys + rows
@@ -165,16 +170,16 @@
             return found
         return lax.fori_loop(0, pages, look, jnp.int32(0))
 
-    quarter = rows * group // chunks
-
-    def prefix_part(side, block, which):
+    tile = min(128, rows * group)
+
+    def prefix_part(side, block, head):
         columns = lax.broadcasted_iota(jnp.int32, (1, keys), 1)
         live = jnp.zeros((1, keys), jnp.int32)
         for s in range(slots):
             inside = (columns >= s * page) & (columns < (s + 1) * page)
             live = jnp.where(inside, slot_live(block * slots + s), live)
-        at = pl.ds(which * quarter, quarter)
-        for head in range(kv_heads):
+        for start in range(0, rows * group, tile):
+            at = slice(start, start + tile)
             scores = lax.dot_general(
                 qs[head, at, :], kx[side, head], (((1,), (1,)), ((), ())),
                 preferred_element_type=jnp.float32,
@@ -183,30 +188,23 @@
             before = m_ref[head, at, :]
             top = jnp.maximum(before, jnp.max(scores, axis=1, keepdims=True))
             factor = jnp.exp2((before - top) * scale)
-            weights = jnp.exp2((scores - top[:, :1]) * scale).astype(jnp.bfloat16)
+            wide = top if keys == depth else top[:, :1]
+            weights = jnp.exp2((scores - wide) * scale).astype(jnp.bfloat16)
             added = jnp.dot(weights, vx[side, head], preferred_element_type=jnp.float32)
             acc_ref[head, at, :depth] = acc_ref[head, at, :depth] * factor + added[:, :depth]
             acc_ref[head, at, depth:] = acc_ref[head, at, depth:] * factor + added[:, depth:]
             m_ref[head, at, :] = top
 
-    def absorb(step, which):
-        if isinstance(step, int) and step == 0:
-            if which == 0:
-                prepare(0, me)
-            prefix_part(0, me, which)
-            return
-
-        @pl.when(me - step >= 0)
-        def _():
-            if which == 0:
-                prepare(0, me - step)
-            prefix_part(0, me - step, which)
-
-        @pl.when(me + step < n)
-        def _():
-            if which == 0:
-                prepare(1, me + step)
-            prefix_part(1, me + step, which)
+    def absorb(step, side, head):
+        block = me - step if side == 0 else me + step
+
+        @pl.when((block >= 0) & (block < n))
+        def _():
+            if head == 0:
+                prepare(side, block)
+            prefix_part(side, block, head)
+
+    pieces = [(side, head) for side in range(2) for head in range(kv_heads)]
 
     for side in range(2):
         for head in range(kv_heads):
@@ -221,20 +219,24 @@
             suffix_block(first + index)
             return carry
 
-        lax.fori_loop(0, count, body, 0)
+        lax.fori_loop(0, count, body, 0, unroll=min(count, 2))
 
     run_suffix(0, suffix_blocks - late * chunks)
     copies[3].wait()
     for chunk in range(chunks):
         relay(1, chunk)
         run_suffix(suffix_blocks - late * (chunks - chunk), late)
-    for chunk in range(chunks):
-        absorb(0, chunk)
+    prepare(0, me)
+    for head in range(kv_heads):
+        prefix_part(0, me, head)
 
     def step_body(step):
         for chunk in range(chunks):
             relay(step, chunk)
-            absorb(step - 1, chunk)
+            low = chunk * len(pieces) // chunks
+            high = (chunk + 1) * len(pieces) // chunks
+            for side, head in pieces[low:high]:
+                absorb(step - 1, side, head)
 
     if n <= 8:
         for step in range(2, n):
@@ -245,9 +247,10 @@
             return carry
 
         lax.fori_loop(2, n, loop, 0)
-    for chunk in range(chunks):
-        absorb(n - 1, chunk)
-
+    for side, head in pieces:
+        absorb(n - 1, side, head)
+
+    quarter = rows * group // chunks
     span = rows // chunks
     count = count_ref[0]
     for chunk in range(chunks):
@@ -282,6 +285,12 @@
         lax.fori_loop(0, n, drain_loop, 0)
 
 
+def store(held, out_hbm, sem):
+    copy = pltpu.make_async_copy(held, out_hbm, sem)
+    copy.start()
+    copy.wait()
+
+
 def shards(n, queries, prefix_pool, page_table, suffix_kv, new_kv, suffix_len, counts):
     rows, heads, depth = queries.shape
     slots, page, pair, kv_heads, depth = prefix_pool.shape
@@ -294,15 +303,18 @@
     new = new_kv.reshape(rows * 2 * kv_heads, depth)
     tile_rows = page * 2 * kv_heads
     bf, f32 = jnp.bfloat16, jnp.float32
-    anywhere = pl.BlockSpec(memory_space=pl.ANY)
-    scalars = pl.BlockSpec(memory_space=pltpu.SMEM)
-    return pl.pallas_call(
+    anywhere = pl.BlockSpec(memory_space=pltpu.HBM)
+    limit = 67043328 - rows * heads * depth * 2
+    result = pl.pallas_call(
         functools.partial(kernel, n, dims),
         name="attend",
-        out_shape=jax.ShapeDtypeStruct((rows, heads, depth), bf),
-        in_specs=[scalars] * 3 + [anywhere] * 4,
+        out_shape=pltpu.VMEM((rows, heads, depth), bf),
+        in_specs=[anywhere] * 7,
         out_specs=pl.BlockSpec(memory_space=pltpu.VMEM),
         scratch_shapes=[
+            pltpu.SMEM(page_table.shape, jnp.int32),
+            pltpu.SMEM(suffix_len.shape, jnp.int32),
+            pltpu.SMEM(counts.shape, jnp.int32),
             pltpu.VMEM((n,) + pool.shape, bf),
             pltpu.VMEM(queries.shape, bf),
             pltpu.VMEM(suffix.shape, bf),
@@ -315,12 +327,23 @@
             pltpu.VMEM((2, kv_heads, slots * page, 2 * depth), bf),
             pltpu.VMEM((kv_heads, rows * group, depth), f32),
             pltpu.VMEM((kv_heads, rows * group, 2 * depth), f32),
-            pltpu.SemaphoreType.DMA((4,)),
+            pltpu.SemaphoreType.DMA((7,)),
             pltpu.SemaphoreType.DMA((2, n, chunks)),
             pltpu.SemaphoreType.DMA((n, chunks)),
         ],
-        compiler_params=pltpu.CompilerParams(collective_id=0, has_side_effects=True),
+        compiler_params=pltpu.CompilerParams(
+            collective_id=0, has_side_effects=True, vmem_limit_bytes=limit
+        ),
     )(page_table, suffix_len, counts, queries, pool, suffix, new)
+    return pl.pallas_call(
+        store,
+        name="store",
+        out_shape=jax.ShapeDtypeStruct((rows, heads, depth), bf),
+        in_specs=[pl.BlockSpec(memory_space=pltpu.VMEM)],
+        out_specs=pl.BlockSpec(memory_space=pltpu.HBM),
+        scratch_shapes=[pltpu.SemaphoreType.DMA],
+        compiler_params=pltpu.CompilerParams(vmem_limit_bytes=4 * 2**20),
+    )(result)
 
 
 def solution(mesh):

time: 26.9 us -> 20.2 us (0.75)
  Pallas kernels: 24.4 us -> 19.3 us
  local copies, waits for them, and re-layouts: 1.67 us -> 0 us
    pallas_call x1, Pallas kernels: 24.4 us -> 18.6 us  [shards(): pl.pallas_call(functools.partial(kernel, n, dims), name='attend', out_sha...]
    unnamed x1 -> x0, local copies, waits for them, and re-layouts: 1.67 us -> none
    pallas_call x0 -> x1, Pallas kernels: none -> 0.71 us  [shards(): pl.pallas_call(store, name='store', out_shape=jax.ShapeDtypeStruct((rows,...]
where the time goes in v2:
time: 20.2 us; the launch traced here: 20 us
  Pallas kernels  19.3 us (96%)
  between operations  0.66 us (3%)
    pallas_call x1, Pallas kernels, shards(): pl.pallas_call(functools.partial(kernel, n, dims), name='attend', out_sha...  18.6 us
    pallas_call x1, Pallas kernels, shards(): pl.pallas_call(store, name='store', out_shape=jax.ShapeDtypeStruct((rows,...  0.71 us

profile of v2, /device:TPU:0, one launch (start us, length us, event | category | flops | bytes accessed | tf_op | source)
XLA Modules:
  0.0 20.0 jit_solution(16311201022407714360)
XLA Ops:
  0.7 18.6 %attend.1.held = bf16[64,16,128]{2,1,0:T(8,128)(2,1)S(1)} custom-call(s32[6]{0:T(128)} %table_hbm.1, s32[64]{0:T(128)} %len_hbm.1, s32[1]{0:T(128)S(6)} %copy.8.count_hbm, bf16[64,16,128]{2,1,0:T(8,128)(2,1)} %q_hbm.1, bf16[512,128]{1,0:T(8,128)(2,1)} %bitcast.4, bf16[6144,128]{1,0:T(8,128)(2,1)} %bitcast.3, bf16[256,128]{1,0:T(8,128)(2,1)} %bitcast.5), custom_call_target="tpu_custom_call" | custom-call | tf_op jit(solution)/shard_map/attend/pallas_call | solution.py:308
  19.3 0.7 %store.1 = bf16[64,16,128]{2,1,0:T(8,128)(2,1)} custom-call(bf16[64,16,128]{2,1,0:T(8,128)(2,1)S(1)} %attend.1.held), custom_call_target="tpu_custom_call" | custom-call | tf_op jit(solution)/shard_map/store/pallas_call | solution.py:338

commit v3 on v2

--- a/solution.py
+++ b/solution.py
@@ -14,7 +14,7 @@
 
 
 def kernel(n, dims, table_hbm, len_hbm, count_hbm, q_hbm, pool_hbm, suf_hbm, new_hbm, out_ref,
-           table_ref, len_ref, count_ref, gather, q_in, suf, new, perm, qs, knew, vnew, kx, vx, m_ref, acc_ref,
+           table_ref, len_ref, count_ref, gather, q_in, suf, new, perm, qs, knew, vnew, m_ref, acc_ref,
            local_sem, send_sem, recv_sem):
     rows, heads, kv_heads, depth, suf_len, page, slots, chunks = dims
     group = heads // kv_heads
@@ -152,12 +152,6 @@
             acc_ref[head, at, :] = jnp.dot(weights, value, preferred_element_type=jnp.float32)
             m_ref[head, at, :] = jnp.broadcast_to(top, (part, depth))
 
-    def prepare(side, block):
-        parts = [split(gather[block, s * tile_rows : (s + 1) * tile_rows, :]) for s in range(slots)]
-        for head in range(kv_heads):
-            kx[side, head] = jnp.concatenate([piece(p, 0, head) for p in parts], axis=0)
-            vx[side, head, :, :depth] = jnp.concatenate([piece(p, 1, head) for p in parts], axis=0)
-
     def slot_live(slot):
         def look(at, found):
             return found | (table_ref[at] == slot).astype(jnp.int32)
@@ -172,43 +166,40 @@
 
     tile = min(128, rows * group)
 
-    def prefix_part(side, block, head):
+    def absorb_block(block):
         columns = lax.broadcasted_iota(jnp.int32, (1, keys), 1)
         live = jnp.zeros((1, keys), jnp.int32)
         for s in range(slots):
             inside = (columns >= s * page) & (columns < (s + 1) * page)
             live = jnp.where(inside, slot_live(block * slots + s), live)
-        for start in range(0, rows * group, tile):
-            at = slice(start, start + tile)
-            scores = lax.dot_general(
-                qs[head, at, :], kx[side, head], (((1,), (1,)), ((), ())),
-                preferred_element_type=jnp.float32,
-            )
-            scores = jnp.where(live > 0, scores, masked_score)
-            before = m_ref[head, at, :]
-            top = jnp.maximum(before, jnp.max(scores, axis=1, keepdims=True))
-            factor = jnp.exp2((before - top) * scale)
-            wide = top if keys == depth else top[:, :1]
-            weights = jnp.exp2((scores - wide) * scale).astype(jnp.bfloat16)
-            added = jnp.dot(weights, vx[side, head], preferred_element_type=jnp.float32)
-            acc_ref[head, at, :depth] = acc_ref[head, at, :depth] * factor + added[:, :depth]
-            acc_ref[head, at, depth:] = acc_ref[head, at, depth:] * factor + added[:, depth:]
-            m_ref[head, at, :] = top
-
-    def absorb(step, side, head):
-        block = me - step if side == 0 else me + step
-
-        @pl.when((block >= 0) & (block < n))
-        def _():
-            if head == 0:
-                prepare(side, block)
-            prefix_part(side, block, head)
-
-    pieces = [(side, head) for side in range(2) for head in range(kv_heads)]
-
-    for side in range(2):
+        parts = [split(gather[block, s * tile_rows : (s + 1) * tile_rows, :]) for s in range(slots)]
+        ones = jnp.ones((keys, depth), jnp.bfloat16)
         for head in range(kv_heads):
-            vx[side, head, :, depth:] = jnp.ones((keys, depth), jnp.bfloat16)
+            key = jnp.concatenate([piece(p, 0, head) for p in parts], axis=0)
+            value = jnp.concatenate([piece(p, 1, head) for p in parts], axis=0)
+            value = jnp.concatenate([value, ones], axis=1)
+            for start in range(0, rows * group, tile):
+                at = slice(start, start + tile)
+                scores = lax.dot_general(
+                    qs[head, at, :], key, (((1,), (1,)), ((), ())),
+                    preferred_element_type=jnp.float32,
+                )
+                scores = jnp.where(live > 0, scores, masked_score)
+                before = m_ref[head, at, :]
+                top = jnp.maximum(before, jnp.max(scores, axis=1, keepdims=True))
+                factor = jnp.exp2((before - top) * scale)
+                wide = top if keys == depth else top[:, :1]
+                weights = jnp.exp2((scores - wide) * scale).astype(jnp.bfloat16)
+                added = jnp.dot(weights, value, preferred_element_type=jnp.float32)
+                acc_ref[head, at, :depth] = acc_ref[head, at, :depth] * factor + added[:, :depth]
+                acc_ref[head, at, depth:] = acc_ref[head, at, depth:] * factor + added[:, depth:]
+                m_ref[head, at, :] = top
+
+    def absorb(step):
+        for block in (me - step, me + step):
+            @pl.when((block >= 0) & (block < n))
+            def _():
+                absorb_block(block)
 
     suffix_blocks = rows // SB
     early = suffix_blocks // 2
@@ -226,29 +217,28 @@
     for chunk in range(chunks):
         relay(1, chunk)
         run_suffix(suffix_blocks - late * (chunks - chunk), late)
-    prepare(0, me)
-    for head in range(kv_heads):
-        prefix_part(0, me, head)
-
-    def step_body(step):
+    absorb_block(me)
+
+    def forward(step):
         for chunk in range(chunks):
             relay(step, chunk)
-            low = chunk * len(pieces) // chunks
-            high = (chunk + 1) * len(pieces) // chunks
-            for side, head in pieces[low:high]:
-                absorb(step - 1, side, head)
+
+    if n > 2:
+        forward(2)
+    absorb(1)
+    if n > 2:
+        absorb(2)
+
+    def step_body(step, carry):
+        forward(step)
+        absorb(step)
+        return carry
 
     if n <= 8:
-        for step in range(2, n):
-            step_body(step)
+        for step in range(3, n):
+            step_body(step, 0)
     else:
-        def loop(step, carry):
-            step_body(step)
-            return carry
-
-        lax.fori_loop(2, n, loop, 0)
-    for side, head in pieces:
-        absorb(n - 1, side, head)
+        lax.fori_loop(3, n, step_body, 0)
 
     quarter = rows * group // chunks
     span = rows // chunks
@@ -323,8 +313,6 @@
             pltpu.VMEM((kv_heads, rows * group, depth), bf),
             pltpu.VMEM((kv_heads, rows, depth), bf),
             pltpu.VMEM((kv_heads, rows, depth), bf),
-            pltpu.VMEM((2, kv_heads, slots * page, depth), bf),
-            pltpu.VMEM((2, kv_heads, slots * page, 2 * depth), bf),
             pltpu.VMEM((kv_heads, rows * group, depth), f32),
             pltpu.VMEM((kv_heads, rows * group, 2 * depth), f32),
             pltpu.SemaphoreType.DMA((7,)),

time: 20.2 us -> 17.8 us (0.88)
  Pallas kernels: 19.3 us -> 17 us
    pallas_call x1, Pallas kernels: 18.6 us -> 16.3 us  [shards(): pl.pallas_call(functools.partial(kernel, n, dims), name='attend', out_sha...]
where the time goes in v3:
time: 17.8 us; the launch traced here: 17.7 us
  Pallas kernels  17 us (96%)
  between operations  0.66 us (4%)
    pallas_call x1, Pallas kernels, shards(): pl.pallas_call(functools.partial(kernel, n, dims), name='attend', out_sha...  16.3 us
    pallas_call x1, Pallas kernels, shards(): pl.pallas_call(store, name='store', out_shape=jax.ShapeDtypeStruct((rows,...  0.71 us

profile of v3, /device:TPU:0, one launch (start us, length us, event | category | flops | bytes accessed | tf_op | source)
XLA Modules:
  0.0 17.7 jit_solution(11115653317405842710)
XLA Ops:
  0.7 16.3 %attend.1.held = bf16[64,16,128]{2,1,0:T(8,128)(2,1)S(1)} custom-call(s32[6]{0:T(128)} %table_hbm.1, s32[64]{0:T(128)} %len_hbm.1, s32[1]{0:T(128)S(6)} %copy.8.count_hbm, bf16[64,16,128]{2,1,0:T(8,128)(2,1)} %q_hbm.1, bf16[512,128]{1,0:T(8,128)(2,1)} %bitcast.4, bf16[6144,128]{1,0:T(8,128)(2,1)} %bitcast.3, bf16[256,128]{1,0:T(8,128)(2,1)} %bitcast.5), custom_call_target="tpu_custom_call" | custom-call | tf_op jit(solution)/shard_map/attend/pallas_call | solution.py:298
  16.9 0.7 %store.1 = bf16[64,16,128]{2,1,0:T(8,128)(2,1)} custom-call(bf16[64,16,128]{2,1,0:T(8,128)(2,1)S(1)} %attend.1.held), custom_call_target="tpu_custom_call" | custom-call | tf_op jit(solution)/shard_map/store/pallas_call | solution.py:326

commit v4 on v3

--- a/solution.py
+++ b/solution.py
@@ -210,7 +210,7 @@
             suffix_block(first + index)
             return carry
 
-        lax.fori_loop(0, count, body, 0, unroll=min(count, 2))
+        lax.fori_loop(0, count, body, 0, unroll=min(count, 4))
 
     run_suffix(0, suffix_blocks - late * chunks)
     copies[3].wait()

time: 17.8 us -> 17.8 us (level)
  no operation moved by 1% of the time
where the time goes in v4:
time: 17.8 us; the launch traced here: 17.7 us
  Pallas kernels  17 us (96%)
  between operations  0.66 us (4%)
    pallas_call x1, Pallas kernels, shards(): pl.pallas_call(functools.partial(kernel, n, dims), name='attend', out_sha...  16.3 us
    pallas_call x1, Pallas kernels, shards(): pl.pallas_call(store, name='store', out_shape=jax.ShapeDtypeStruct((rows,...  0.71 us

profile of v4, /device:TPU:0, one launch (start us, length us, event | category | flops | bytes accessed | tf_op | source)
XLA Modules:
  0.0 17.7 jit_solution(12135139399125367044)
XLA Ops:
  0.7 16.3 %attend.1.held = bf16[64,16,128]{2,1,0:T(8,128)(2,1)S(1)} custom-call(s32[6]{0:T(128)} %table_hbm.1, s32[64]{0:T(128)} %len_hbm.1, s32[1]{0:T(128)S(6)} %copy.8.count_hbm, bf16[64,16,128]{2,1,0:T(8,128)(2,1)} %q_hbm.1, bf16[512,128]{1,0:T(8,128)(2,1)} %bitcast.4, bf16[6144,128]{1,0:T(8,128)(2,1)} %bitcast.3, bf16[256,128]{1,0:T(8,128)(2,1)} %bitcast.5), custom_call_target="tpu_custom_call" | custom-call | tf_op jit(solution)/shard_map/attend/pallas_call | solution.py:298
  16.9 0.7 %store.1 = bf16[64,16,128]{2,1,0:T(8,128)(2,1)} custom-call(bf16[64,16,128]{2,1,0:T(8,128)(2,1)S(1)} %attend.1.held), custom_call_target="tpu_custom_call" | custom-call | tf_op jit(solution)/shard_map/store/pallas_call | solution.py:326
